TPU v7x, 32 devices: a whole 2x2x4 slice. The times are simulated.
32 devices in a mesh: gx: 4 (over x, core), gy: 8 (over z, y).
Axes of the slice: x: 2, y: 2, z: 4, core: 2. Of those that a mesh axis runs over, the one named last changes fastest.
Arguments:
- probes: float32 [32, 64, 64, 256], P(None, 'gx', 'gy'), may hold values from -108 to 108, as said below
- diffusion: float32 [64, 64, 256], P('gx', 'gy'), may hold values from 0.03 to 0.16
- velocity: float32 [3, 64, 64, 256], P(None, 'gx', 'gy'), may hold values from -0.2 to 0.2
Outputs:
- basis: float32 [32, 64, 64, 256], P(None, 'gx', 'gy')
- factor: float32 [32, 32], replicated
Inputs may be any that keep to these rules, and one draw needn't show every extreme that they name: `probes`: each entry is finite and real-valued.
All inputs are finite; a program needn't handle non-finite values.
Results may differ from a plain program's by a relative error of at most 0.00011.
Values sent between devices are 32-bit elements; how exact they have to be, the bound alone decides.
No kernel may reach another device: no remote copies, remote signals or barrier semaphores. Data moves between devices by JAX's collectives and lax.ppermute only.
A program may use at most 64 MiB of HBM per device.

v0:
```python
import jax
import jax.numpy as jnp
from jax import lax
from jax.sharding import PartitionSpec as P

STEPS = 2


def with_halo(cells, sides, width):
    for axis, dim in sides:
        count = lax.axis_size(axis)
        ends = count - 1
        head = lax.slice_in_dim(cells, 0, width, axis=dim)
        tail = lax.slice_in_dim(cells, cells.shape[dim] - width, cells.shape[dim], axis=dim)
        cells = jnp.concatenate(
            [
                lax.ppermute(tail, axis, [(i, (i + 1) % count) for i in range(ends)]),
                cells,
                lax.ppermute(head, axis, [((i + 1) % count, i) for i in range(ends)]),
            ],
            axis=dim,
        )
    return cells


def stencil_step(padded, diffusion, velocity):
    center = padded[:, 1:-1, 1:-1, :]
    deeper = jnp.pad(center, ((0, 0), (0, 0), (0, 0), (1, 1)))
    result = (1.0 - 6.0 * diffusion) * center
    result = (
        result
        + (diffusion - 0.5 * velocity[0]) * padded[:, 2:, 1:-1, :]
        + (diffusion + 0.5 * velocity[0]) * padded[:, :-2, 1:-1, :]
    )
    result = (
        result
        + (diffusion - 0.5 * velocity[1]) * padded[:, 1:-1, 2:, :]
        + (diffusion + 0.5 * velocity[1]) * padded[:, 1:-1, :-2, :]
    )
    result = (
        result
        + (diffusion - 0.5 * velocity[2]) * deeper[:, :, :, 2:]
        + (diffusion + 0.5 * velocity[2]) * deeper[:, :, :, :-2]
    )
    return result


def on_device(probes, diffusion, velocity):
    field = probes
    for sweep_index in range(STEPS):
        padded = with_halo(field, (("gx", 1), ("gy", 2)), 1)
        field = stencil_step(padded, diffusion, velocity)
    probe_count = field.shape[0]
    flat = field.reshape(probe_count, -1)
    total_cells = flat.shape[1] * lax.axis_size("gx") * lax.axis_size("gy")
    local_gram = jnp.dot(
        flat, flat.T, precision=lax.Precision.HIGHEST, preferred_element_type=jnp.float32
    )
    gram = lax.psum(local_gram, ("gx", "gy")) * (1.0 / total_cells)
    lower = jnp.linalg.cholesky(gram)
    basis = jax.scipy.linalg.solve_triangular(lower, flat, lower=True)
    return (basis.reshape(field.shape), lower.T)


def solution(mesh):
    return jax.shard_map(
        on_device,
        mesh=mesh,
        in_specs=(P(None, "gx", "gy", None), P("gx", "gy", None), P(None, "gx", "gy", None)),
        out_specs=(P(None, "gx", "gy", None), P()),
        check_vma=False,
    )
```

profile of v0, /device:TPU:0, one launch (start us, length us, event | category | flops | bytes accessed | tf_op | source)
XLA Modules:
  0.0 177.1 jit_solution(3824144828677573553)
XLA Ops:
  0.6 4.8 %copy.33 = f32[32,16,8,256]{3,0,2,1:T(8,128)S(1)} copy(f32[32,16,8,256]{3,2,1,0:T(8,128)} %param.3) | data formatting | bytes 8388608 | tf_op args[0]
  5.5 2.4 %collective-permute-start.1 = (f32[32,1,8,256]{3,0,2,1:T(8,128)S(1)}, f32[32,1,8,256]{3,0,2,1:T(8,128)S(1)}, u32[]{:S(2)}, u32[]{:S(2)}) collective-permute-start(f32[32,1,8,256]{3,0,2,1:T(8,128)S(1)} %get-tuple-element.17), channel_id=1, source_target_pairs={{0,8},{8,16},{16,24},{1,9},{9,17},{17,25},{2,10},{10,18},{18,26},{... | collective-permute-start | bytes 786440 | tf_op jit(solution)/shard_map/ppermute | solution.py:17
  7.8 1.3 collective-permute-start
  9.2 2.7 %constant_dynamic-update-slice_fusion.1 = f32[32,18,8,256]{3,0,2,1:T(8,128)S(1)} fusion(f32[32,18,8,256]{3,0,2,1:T(8,128)S(1)} %constant_dynamic-update-slice_fusion.2, f32[32,16,8,256]{3,2,1,0:T(8,128)S(1)} %copy-done.2), kind=kLoop, calls=%fused_computation.66 | loop fusion | bytes 8388608
  11.9 1.4 collective-permute-done
  13.4 0.1 fusion.29
  13.5 1.3 collective-permute-start.2
  14.8 4.6 %collective-permute-start.3 = (f32[32,18,1,256]{3,0,2,1:T(8,128)S(1)}, f32[32,18,1,256]{3,0,2,1:T(8,128)S(1)}, u32[]{:S(2)}, u32[]{:S(2)}) collective-permute-start(f32[32,18,1,256]{3,0,2,1:T(8,128)S(1)} %get-tuple-element.13), channel_id=1, source_target_pairs={{0,1},{1,2},{2,3},{3,4},{4,5},{5,6},{6,7},{8,9},{9,10},{10,11},{11... | collective-permute-start | bytes 1769480 | tf_op jit(solution)/shard_map/ppermute | solution.py:17
  19.4 0.1 bitcast_subtract_fusion.2
  19.5 8.2 %collective-permute-done.2 = f32[32,18,1,256]{3,0,2,1:T(8,128)S(1)} collective-permute-done((f32[32,18,1,256]{3,0,2,1:T(8,128)S(1)}, f32[32,18,1,256]{3,0,2,1:T(8,128)S(1)}, u32[]{:S(2)}, u32[]{:S(2)}) %collective-permute-start.2) | collective-permute-done | bytes 589856 | tf_op jit(solution)/shard_map/ppermute | solution.py:19
  27.7 16.3 %collective-permute-done.3 = f32[32,18,1,256]{3,0,2,1:T(8,128)S(1)} collective-permute-done((f32[32,18,1,256]{3,0,2,1:T(8,128)S(1)}, f32[32,18,1,256]{3,0,2,1:T(8,128)S(1)}, u32[]{:S(2)}, u32[]{:S(2)}) %collective-permute-start.3) | collective-permute-done | bytes 589856 | tf_op jit(solution)/shard_map/ppermute | solution.py:17
  44.1 9.5 %fusion.2 = f32[32,16,8,256]{3,0,2,1:T(8,128)S(1)} fusion(f32[32,16,8,256]{3,0,2,1:T(8,128)S(1)} %copy.33, f32[32,18,8,256]{3,0,2,1:T(8,128)} %copy-done.3, f32[32,18,1,256]{3,0,2,1:T(8,128)S(1)} %collective-permute-done.3, f32[32,18,1,256]{3,0,2,1:T(8,128)S(1)} %collective-permute-done.2, f32[32,1,8,256]{3,0,2,1:T(8,128)S(1)} %collective-permute-done.1, ...), kind=kLoop, calls=%fused_computation.6 | loop fusion | flops 17825792 | bytes 15728640 | tf_op jit(solution)/shard_map/add | solution.py:41
  53.6 2.2 %collective-permute-start.5 = (f32[32,1,8,256]{3,0,2,1:T(8,128)S(1)}, f32[32,1,8,256]{3,0,2,1:T(8,128)S(1)}, u32[]{:S(2)}, u32[]{:S(2)}) collective-permute-start(f32[32,1,8,256]{3,0,2,1:T(8,128)S(1)} %get-tuple-element.14), channel_id=1, source_target_pairs={{0,8},{8,16},{16,24},{1,9},{9,17},{17,25},{2,10},{10,18},{18,26},{... | collective-permute-start | bytes 786440 | tf_op jit(solution)/shard_map/ppermute | solution.py:17
  55.8 1.3 collective-permute-start.4
  57.1 2.7 %collective-permute-done.4 = f32[32,1,8,256]{3,0,2,1:T(8,128)S(1)} collective-permute-done((f32[32,1,8,256]{3,0,2,1:T(8,128)S(1)}, f32[32,1,8,256]{3,0,2,1:T(8,128)S(1)}, u32[]{:S(2)}, u32[]{:S(2)}) %collective-permute-start.4) | collective-permute-done | bytes 262176 | tf_op jit(solution)/shard_map/ppermute | solution.py:19
  59.9 0.1 pad_maximum_fusion.14
  60.0 1.3 collective-permute-start.6
  61.3 5.2 %collective-permute-start.7 = (f32[32,18,1,256]{3,0,2,1:T(8,128)S(1)}, f32[32,18,1,256]{3,0,2,1:T(8,128)S(1)}, u32[]{:S(2)}, u32[]{:S(2)}) collective-permute-start(f32[32,18,1,256]{3,0,2,1:T(8,128)S(1)} %get-tuple-element.11), channel_id=1, source_target_pairs={{0,1},{1,2},{2,3},{3,4},{4,5},{5,6},{6,7},{8,9},{9,10},{10,11},{11... | collective-permute-start | bytes 1769480 | tf_op jit(solution)/shard_map/ppermute | solution.py:17
  66.5 7.9 %collective-permute-done.6 = f32[32,18,1,256]{3,0,2,1:T(8,128)S(1)} collective-permute-done((f32[32,18,1,256]{3,0,2,1:T(8,128)S(1)}, f32[32,18,1,256]{3,0,2,1:T(8,128)S(1)}, u32[]{:S(2)}, u32[]{:S(2)}) %collective-permute-start.6) | collective-permute-done | bytes 589856 | tf_op jit(solution)/shard_map/ppermute | solution.py:19
  74.4 17.1 %collective-permute-done.7 = f32[32,18,1,256]{3,0,2,1:T(8,128)S(1)} collective-permute-done((f32[32,18,1,256]{3,0,2,1:T(8,128)S(1)}, f32[32,18,1,256]{3,0,2,1:T(8,128)S(1)}, u32[]{:S(2)}, u32[]{:S(2)}) %collective-permute-start.7) | collective-permute-done | bytes 589856 | tf_op jit(solution)/shard_map/ppermute | solution.py:17
  91.5 17.3 %fusion.6 = f32[32,16,8,256]{3,0,2,1:T(8,128)S(1)} fusion(f32[32,16,8,256]{3,0,2,1:T(8,128)} %copy-done.1, f32[32,18,1,256]{3,0,2,1:T(8,128)S(1)} %collective-permute-done.7, f32[32,1,8,256]{3,0,2,1:T(8,128)S(1)} %collective-permute-done.4, f32[32,1,8,256]{3,0,2,1:T(8,128)S(1)} %collective-permute-done.5, f32[32,18,1,256]{3,0,2,1:T(8,128)S(1)} %collective-permute-done.6, ...), kind=kLoop, calls=%fused_computation.10 | loop fusion | flops 22020096 | bytes 11010048 | tf_op jit(solution)/shard_map/add | solution.py:41
  108.9 2.0 %copy-done = f32[32,16,8,256]{3,0,2,1:T(8,128)} copy-done((f32[32,16,8,256]{3,0,2,1:T(8,128)}, f32[32,16,8,256]{3,0,2,1:T(8,128)S(1)}, u32[]{:S(2)}) %copy-start) | copy-done | bytes 4194328
  110.9 3.4 %convolution_bitcast_fusion = f32[32,32]{0,1:T(8,128)S(1)} fusion(f32[32,16,8,256]{3,0,2,1:T(8,128)S(1)} %fusion.6), kind=kOutput, calls=%fused_computation.42 | convolution fusion | flops 402653184 | bytes 4198400 | tf_op jit(solution)/shard_map/dot_general | solution.py:56
  114.3 40.3 %psum.7 = f32[32,32]{0,1:T(8,128)S(1)} all-reduce(f32[32,32]{0,1:T(8,128)S(1)} %convolution_bitcast_fusion), channel_id=1, replica_groups=mesh['gx'=4,'gy'=8] {'gx','gy'}, use_global_device_ids=true, to_apply=%region_0.1 | all-reduce | flops 1024 | bytes 8192 | tf_op jit(solution)/shard_map/psum | solution.py:59
  154.7 2.9 %cholesky.16 = f32[32,32]{1,0:T(8,128)S(1)} custom-call(f32[32,32]{1,0:T(8,128)S(1)} %fusion.27), custom_call_target="Cholesky" | custom-call | tf_op jit(solution)/shard_map/jit(cholesky)/cholesky | solution.py:60
  157.7 0.6 compare_reduce_fusion
  158.3 0.7 fusion.28
  159.0 0.7 copy.46
  159.6 2.4 %custom-call.7 = f32[1,32,32]{1,2,0:T(8,128)S(1)} custom-call(f32[1,32,32]{2,1,0:T(8,128)S(1)} %get-tuple-element.26), custom_call_target="InvertDiagBlocksLowerTriangular" | custom-call | tf_op jit(solution)/shard_map/jit(_solve_triangular)/triangular_solve | solution.py:61
  162.1 4.6 %copy.52 = f32[4,8,128,256]{3,2,1,0:T(8,128)S(1)} copy(f32[4,8,128,256]{3,1,0,2:T(8,128)} %bitcast.37) | data formatting | bytes 8388608
  166.7 5.9 %fusion.24 = f32[32,16,8,256]{3,0,2,1:T(8,128)S(1)} fusion(f32[16,8,256,32]{2,1,0,3:T(8,128)S(1)} %bitcast.38, f32[1,32,32]{1,2,0:T(8,128)S(1)} %custom-call.7), kind=kOutput, calls=%fused_computation.40 | convolution fusion | flops 402653184 | bytes 8392704 | tf_op jit(solution)/shard_map/jit(_solve_triangular)/triangular_solve | solution.py:61
  172.7 4.4 %copy.45 = f32[32,16,8,256]{3,2,1,0:T(8,128)} copy(f32[32,16,8,256]{3,0,2,1:T(8,128)S(1)} %fusion.24) | data formatting | bytes 8388608
  (21 shorter events, 0.3 us)
Async XLA Ops:
  0.6 8.5 %copy-start.2 = (f32[32,16,8,256]{3,2,1,0:T(8,128)S(1)}, f32[32,16,8,256]{3,2,1,0:T(8,128)}, u32[]{:S(2)}) copy-start(f32[32,16,8,256]{3,2,1,0:T(8,128)} %param.3) | copy-start | bytes 12582916
  5.5 3.7 %collective-permute-start.1 = (f32[32,1,8,256]{3,0,2,1:T(8,128)S(1)}, f32[32,1,8,256]{3,0,2,1:T(8,128)S(1)}, u32[]{:S(2)}, u32[]{:S(2)}) collective-permute-start(f32[32,1,8,256]{3,0,2,1:T(8,128)S(1)} %get-tuple-element.17), channel_id=1, source_target_pairs={{0,8},{8,16},{16,24},{1,9},{9,17},{17,25},{2,10},{10,18},{18,26},{... | collective-permute-start | bytes 786440 | tf_op jit(solution)/shard_map/ppermute | solution.py:17
  7.8 5.5 %collective-permute-start = (f32[32,1,8,256]{3,0,2,1:T(8,128)S(1)}, f32[32,1,8,256]{3,0,2,1:T(8,128)S(1)}, u32[]{:S(2)}, u32[]{:S(2)}) collective-permute-start(f32[32,1,8,256]{3,0,2,1:T(8,128)S(1)} %get-tuple-element.16), channel_id=1, source_target_pairs={{8,0},{16,8},{24,16},{9,1},{17,9},{25,17},{10,2},{18,10},{26,18},{... | collective-permute-start | bytes 786440 | tf_op jit(solution)/shard_map/ppermute | solution.py:19
  9.2 10.2 %copy-start.4 = (f32[3,16,8,256]{3,2,1,0:T(8,128)S(1)}, f32[3,16,8,256]{3,2,1,0:T(8,128)}, u32[]{:S(2)}) copy-start(f32[3,16,8,256]{3,2,1,0:T(8,128)} %param.5) | copy-start | bytes 1179652
  9.2 10.2 %copy-start.5 = (f32[16,8,256]{2,1,0:T(8,128)S(1)}, f32[16,8,256]{2,1,0:T(8,128)}, u32[]{:S(2)}) copy-start(f32[16,8,256]{2,1,0:T(8,128)} %param.4) | copy-start | bytes 393220
  13.4 30.7 %copy-start.3 = (f32[32,18,8,256]{3,0,2,1:T(8,128)}, f32[32,18,8,256]{3,0,2,1:T(8,128)S(1)}, u32[]{:S(2)}) copy-start(f32[32,18,8,256]{3,0,2,1:T(8,128)S(1)} %constant_dynamic-update-slice_fusion) | copy-start | bytes 14155780
  13.5 14.2 %collective-permute-start.2 = (f32[32,18,1,256]{3,0,2,1:T(8,128)S(1)}, f32[32,18,1,256]{3,0,2,1:T(8,128)S(1)}, u32[]{:S(2)}, u32[]{:S(2)}) collective-permute-start(f32[32,18,1,256]{3,0,2,1:T(8,128)S(1)} %get-tuple-element.12), channel_id=1, source_target_pairs={{1,0},{2,1},{3,2},{4,3},{5,4},{6,5},{7,6},{9,8},{10,9},{11,10},{12... | collective-permute-start | bytes 1769480 | tf_op jit(solution)/shard_map/ppermute | solution.py:19
  14.8 29.3 %collective-permute-start.3 = (f32[32,18,1,256]{3,0,2,1:T(8,128)S(1)}, f32[32,18,1,256]{3,0,2,1:T(8,128)S(1)}, u32[]{:S(2)}, u32[]{:S(2)}) collective-permute-start(f32[32,18,1,256]{3,0,2,1:T(8,128)S(1)} %get-tuple-element.13), channel_id=1, source_target_pairs={{0,1},{1,2},{2,3},{3,4},{4,5},{5,6},{6,7},{8,9},{9,10},{10,11},{11... | collective-permute-start | bytes 1769480 | tf_op jit(solution)/shard_map/ppermute | solution.py:17
  53.5 20.9 %copy-start.1 = (f32[32,16,8,256]{3,0,2,1:T(8,128)}, f32[32,16,8,256]{3,0,2,1:T(8,128)S(1)}, u32[]{:S(2)}) copy-start(f32[32,16,8,256]{3,0,2,1:T(8,128)S(1)} %fusion.2) | copy-start | bytes 12582916
  53.6 3.5 %collective-permute-start.5 = (f32[32,1,8,256]{3,0,2,1:T(8,128)S(1)}, f32[32,1,8,256]{3,0,2,1:T(8,128)S(1)}, u32[]{:S(2)}, u32[]{:S(2)}) collective-permute-start(f32[32,1,8,256]{3,0,2,1:T(8,128)S(1)} %get-tuple-element.14), channel_id=1, source_target_pairs={{0,8},{8,16},{16,24},{1,9},{9,17},{17,25},{2,10},{10,18},{18,26},{... | collective-permute-start | bytes 786440 | tf_op jit(solution)/shard_map/ppermute | solution.py:17
  55.8 4.1 %collective-permute-start.4 = (f32[32,1,8,256]{3,0,2,1:T(8,128)S(1)}, f32[32,1,8,256]{3,0,2,1:T(8,128)S(1)}, u32[]{:S(2)}, u32[]{:S(2)}) collective-permute-start(f32[32,1,8,256]{3,0,2,1:T(8,128)S(1)} %get-tuple-element.15), channel_id=1, source_target_pairs={{8,0},{16,8},{24,16},{9,1},{17,9},{25,17},{10,2},{18,10},{26,18},{... | collective-permute-start | bytes 786440 | tf_op jit(solution)/shard_map/ppermute | solution.py:19
  60.0 14.4 %collective-permute-start.6 = (f32[32,18,1,256]{3,0,2,1:T(8,128)S(1)}, f32[32,18,1,256]{3,0,2,1:T(8,128)S(1)}, u32[]{:S(2)}, u32[]{:S(2)}) collective-permute-start(f32[32,18,1,256]{3,0,2,1:T(8,128)S(1)} %get-tuple-element.10), channel_id=1, source_target_pairs={{1,0},{2,1},{3,2},{4,3},{5,4},{6,5},{7,6},{9,8},{10,9},{11,10},{12... | collective-permute-start | bytes 1769480 | tf_op jit(solution)/shard_map/ppermute | solution.py:19
  61.3 30.2 %collective-permute-start.7 = (f32[32,18,1,256]{3,0,2,1:T(8,128)S(1)}, f32[32,18,1,256]{3,0,2,1:T(8,128)S(1)}, u32[]{:S(2)}, u32[]{:S(2)}) collective-permute-start(f32[32,18,1,256]{3,0,2,1:T(8,128)S(1)} %get-tuple-element.11), channel_id=1, source_target_pairs={{0,1},{1,2},{2,3},{3,4},{4,5},{5,6},{6,7},{8,9},{9,10},{10,11},{11... | collective-permute-start | bytes 1769480 | tf_op jit(solution)/shard_map/ppermute | solution.py:17
  108.9 2.0 %copy-start = (f32[32,16,8,256]{3,0,2,1:T(8,128)}, f32[32,16,8,256]{3,0,2,1:T(8,128)S(1)}, u32[]{:S(2)}) copy-start(f32[32,16,8,256]{3,0,2,1:T(8,128)S(1)} %fusion.6) | copy-start | bytes 12582916
where the time goes:
time: 178 us; the launch traced here: 177 us
  waiting for transfers between devices  53.8 us (30%)
  blocking collectives  40.3 us (23%)
  other arithmetic  33.7 us (19%)
  local copies, waits for them, and re-layouts  19.6 us (11%)
  starting transfers between devices  19.6 us (11%)
  matrix products  9.3 us (5%)
    psum x1, blocking collectives, on_device(): gram = lax.psum(local_gram, ('gx', 'gy')) * (1.0 / total_cells)  40.3 us
    ppermute x4, waiting for transfers between devices, with_halo(): lax.ppermute(tail, axis, [(i, (i + 1) % count) for i in range(ends)])  33.4 us
    add x2, other arithmetic, stencil_step(): result + (diffusion - 0.5 * velocity[2]) * deeper[:, :, :, 2:]  26.8 us
    ppermute x4, waiting for transfers between devices, with_halo(): lax.ppermute(head, axis, [((i + 1) % count, i) for i in range(ends)])  20.3 us
    unnamed x18, local copies, waits for them, and re-layouts  19.3 us
    ppermute x4, starting transfers between devices, with_halo(): lax.ppermute(tail, axis, [(i, (i + 1) % count) for i in range(ends)])  14.4 us
    another operation x1, matrix products, on_device(): basis = jax.scipy.linalg.solve_triangular(lower, flat, lower=True)  5.92 us
    ppermute x4, starting transfers between devices, with_halo(): lax.ppermute(head, axis, [((i + 1) % count, i) for i in range(ends)])  5.17 us
  transfers between devices with their start and end apart: 8, of which 6 were waited for; matrix products, arithmetic and copies ran while one was open for 2% of the time, Pallas kernels for 0%

commit v1 on v0

--- a/solution.py
+++ b/solution.py
@@ -56,7 +56,7 @@
     local_gram = jnp.dot(
         flat, flat.T, precision=lax.Precision.HIGHEST, preferred_element_type=jnp.float32
     )
-    gram = lax.psum(local_gram, ("gx", "gy")) * (1.0 / total_cells)
+    gram = lax.psum(lax.psum(local_gram, "gy"), "gx") * (1.0 / total_cells)
     lower = jnp.linalg.cholesky(gram)
     basis = jax.scipy.linalg.solve_triangular(lower, flat, lower=True)
     return (basis.reshape(field.shape), lower.T)

time: 178 us -> 183 us (1.028)
  blocking collectives: 40.3 us -> 45.9 us
    psum x1 -> x2, blocking collectives: 40.3 us -> 45.9 us  [on_device(): gram = lax.psum(lax.psum(local_gram, 'gy'), 'gx') * (1.0 / total_cells)]
where the time goes in v1:
time: 183 us
  waiting for transfers between devices  53.8 us (29%)
  blocking collectives  45.9 us (25%)
  other arithmetic  33.7 us (18%)
  local copies, waits for them, and re-layouts  19.6 us (11%)
  starting transfers between devices  19.6 us (11%)
  matrix products  9.3 us (5%)
    psum x2, blocking collectives, on_device(): gram = lax.psum(lax.psum(local_gram, 'gy'), 'gx') * (1.0 / total_cells)  45.9 us
    ppermute x4, waiting for transfers between devices, with_halo(): lax.ppermute(tail, axis, [(i, (i + 1) % count) for i in range(ends)])  33.4 us
    add x2, other arithmetic, stencil_step(): result + (diffusion - 0.5 * velocity[2]) * deeper[:, :, :, 2:]  26.8 us
    ppermute x4, waiting for transfers between devices, with_halo(): lax.ppermute(head, axis, [((i + 1) % count, i) for i in range(ends)])  20.3 us
    unnamed x18, local copies, waits for them, and re-layouts  19.3 us
    ppermute x4, starting transfers between devices, with_halo(): lax.ppermute(tail, axis, [(i, (i + 1) % count) for i in range(ends)])  14.4 us
    another operation x1, matrix products, on_device(): basis = jax.scipy.linalg.solve_triangular(lower, flat, lower=True)  5.92 us
    ppermute x4, starting transfers between devices, with_halo(): lax.ppermute(head, axis, [((i + 1) % count, i) for i in range(ends)])  5.17 us
  transfers between devices with their start and end apart: 8, of which 6 were waited for; matrix products, arithmetic and copies ran while one was open for 2% of the time, Pallas kernels for 0%

profile of v1, /device:TPU:0, one launch (start us, length us, event | category | flops | bytes accessed | tf_op | source)
XLA Modules:
  0.0 182.6 jit_solution(4213184962818356073)
XLA Ops:
  0.6 4.8 %copy.33 = f32[32,16,8,256]{3,0,2,1:T(8,128)S(1)} copy(f32[32,16,8,256]{3,2,1,0:T(8,128)} %param.3) | data formatting | bytes 8388608 | tf_op args[0]
  5.5 2.4 %collective-permute-start.1 = (f32[32,1,8,256]{3,0,2,1:T(8,128)S(1)}, f32[32,1,8,256]{3,0,2,1:T(8,128)S(1)}, u32[]{:S(2)}, u32[]{:S(2)}) collective-permute-start(f32[32,1,8,256]{3,0,2,1:T(8,128)S(1)} %get-tuple-element.17), channel_id=1, source_target_pairs={{0,8},{8,16},{16,24},{1,9},{9,17},{17,25},{2,10},{10,18},{18,26},{... | collective-permute-start | bytes 786440 | tf_op jit(solution)/shard_map/ppermute | solution.py:17
  7.8 1.3 collective-permute-start
  9.2 2.7 %constant_dynamic-update-slice_fusion.1 = f32[32,18,8,256]{3,0,2,1:T(8,128)S(1)} fusion(f32[32,18,8,256]{3,0,2,1:T(8,128)S(1)} %constant_dynamic-update-slice_fusion.2, f32[32,16,8,256]{3,2,1,0:T(8,128)S(1)} %copy-done.2), kind=kLoop, calls=%fused_computation.66 | loop fusion | bytes 8388608
  11.9 1.4 collective-permute-done
  13.4 0.1 fusion.29
  13.5 1.3 collective-permute-start.2
  14.8 4.6 %collective-permute-start.3 = (f32[32,18,1,256]{3,0,2,1:T(8,128)S(1)}, f32[32,18,1,256]{3,0,2,1:T(8,128)S(1)}, u32[]{:S(2)}, u32[]{:S(2)}) collective-permute-start(f32[32,18,1,256]{3,0,2,1:T(8,128)S(1)} %get-tuple-element.13), channel_id=1, source_target_pairs={{0,1},{1,2},{2,3},{3,4},{4,5},{5,6},{6,7},{8,9},{9,10},{10,11},{11... | collective-permute-start | bytes 1769480 | tf_op jit(solution)/shard_map/ppermute | solution.py:17
  19.5 8.2 %collective-permute-done.2 = f32[32,18,1,256]{3,0,2,1:T(8,128)S(1)} collective-permute-done((f32[32,18,1,256]{3,0,2,1:T(8,128)S(1)}, f32[32,18,1,256]{3,0,2,1:T(8,128)S(1)}, u32[]{:S(2)}, u32[]{:S(2)}) %collective-permute-start.2) | collective-permute-done | bytes 589856 | tf_op jit(solution)/shard_map/ppermute | solution.py:19
  27.7 16.3 %collective-permute-done.3 = f32[32,18,1,256]{3,0,2,1:T(8,128)S(1)} collective-permute-done((f32[32,18,1,256]{3,0,2,1:T(8,128)S(1)}, f32[32,18,1,256]{3,0,2,1:T(8,128)S(1)}, u32[]{:S(2)}, u32[]{:S(2)}) %collective-permute-start.3) | collective-permute-done | bytes 589856 | tf_op jit(solution)/shard_map/ppermute | solution.py:17
  44.1 9.5 %fusion.2 = f32[32,16,8,256]{3,0,2,1:T(8,128)S(1)} fusion(f32[32,16,8,256]{3,0,2,1:T(8,128)S(1)} %copy.33, f32[32,18,8,256]{3,0,2,1:T(8,128)} %copy-done.3, f32[32,18,1,256]{3,0,2,1:T(8,128)S(1)} %collective-permute-done.3, f32[32,18,1,256]{3,0,2,1:T(8,128)S(1)} %collective-permute-done.2, f32[32,1,8,256]{3,0,2,1:T(8,128)S(1)} %collective-permute-done.1, ...), kind=kLoop, calls=%fused_computation.6 | loop fusion | flops 17825792 | bytes 15728640 | tf_op jit(solution)/shard_map/add | solution.py:41
  53.6 2.2 %collective-permute-start.5 = (f32[32,1,8,256]{3,0,2,1:T(8,128)S(1)}, f32[32,1,8,256]{3,0,2,1:T(8,128)S(1)}, u32[]{:S(2)}, u32[]{:S(2)}) collective-permute-start(f32[32,1,8,256]{3,0,2,1:T(8,128)S(1)} %get-tuple-element.14), channel_id=1, source_target_pairs={{0,8},{8,16},{16,24},{1,9},{9,17},{17,25},{2,10},{10,18},{18,26},{... | collective-permute-start | bytes 786440 | tf_op jit(solution)/shard_map/ppermute | solution.py:17
  55.8 1.3 collective-permute-start.4
  57.1 2.7 %collective-permute-done.4 = f32[32,1,8,256]{3,0,2,1:T(8,128)S(1)} collective-permute-done((f32[32,1,8,256]{3,0,2,1:T(8,128)S(1)}, f32[32,1,8,256]{3,0,2,1:T(8,128)S(1)}, u32[]{:S(2)}, u32[]{:S(2)}) %collective-permute-start.4) | collective-permute-done | bytes 262176 | tf_op jit(solution)/shard_map/ppermute | solution.py:19
  59.9 0.1 pad_maximum_fusion.14
  60.0 1.3 collective-permute-start.6
  61.3 5.2 %collective-permute-start.7 = (f32[32,18,1,256]{3,0,2,1:T(8,128)S(1)}, f32[32,18,1,256]{3,0,2,1:T(8,128)S(1)}, u32[]{:S(2)}, u32[]{:S(2)}) collective-permute-start(f32[32,18,1,256]{3,0,2,1:T(8,128)S(1)} %get-tuple-element.11), channel_id=1, source_target_pairs={{0,1},{1,2},{2,3},{3,4},{4,5},{5,6},{6,7},{8,9},{9,10},{10,11},{11... | collective-permute-start | bytes 1769480 | tf_op jit(solution)/shard_map/ppermute | solution.py:17
  66.5 7.9 %collective-permute-done.6 = f32[32,18,1,256]{3,0,2,1:T(8,128)S(1)} collective-permute-done((f32[32,18,1,256]{3,0,2,1:T(8,128)S(1)}, f32[32,18,1,256]{3,0,2,1:T(8,128)S(1)}, u32[]{:S(2)}, u32[]{:S(2)}) %collective-permute-start.6) | collective-permute-done | bytes 589856 | tf_op jit(solution)/shard_map/ppermute | solution.py:19
  74.4 17.1 %collective-permute-done.7 = f32[32,18,1,256]{3,0,2,1:T(8,128)S(1)} collective-permute-done((f32[32,18,1,256]{3,0,2,1:T(8,128)S(1)}, f32[32,18,1,256]{3,0,2,1:T(8,128)S(1)}, u32[]{:S(2)}, u32[]{:S(2)}) %collective-permute-start.7) | collective-permute-done | bytes 589856 | tf_op jit(solution)/shard_map/ppermute | solution.py:17
  91.5 17.3 %fusion.6 = f32[32,16,8,256]{3,0,2,1:T(8,128)S(1)} fusion(f32[32,16,8,256]{3,0,2,1:T(8,128)} %copy-done.1, f32[32,18,1,256]{3,0,2,1:T(8,128)S(1)} %collective-permute-done.7, f32[32,1,8,256]{3,0,2,1:T(8,128)S(1)} %collective-permute-done.4, f32[32,1,8,256]{3,0,2,1:T(8,128)S(1)} %collective-permute-done.5, f32[32,18,1,256]{3,0,2,1:T(8,128)S(1)} %collective-permute-done.6, ...), kind=kLoop, calls=%fused_computation.10 | loop fusion | flops 22020096 | bytes 11010048 | tf_op jit(solution)/shard_map/add | solution.py:41
  108.9 2.0 %copy-done = f32[32,16,8,256]{3,0,2,1:T(8,128)} copy-done((f32[32,16,8,256]{3,0,2,1:T(8,128)}, f32[32,16,8,256]{3,0,2,1:T(8,128)S(1)}, u32[]{:S(2)}) %copy-start) | copy-done | bytes 4194328
  110.9 3.4 %convolution_bitcast_fusion = f32[32,32]{0,1:T(8,128)S(1)} fusion(f32[32,16,8,256]{3,0,2,1:T(8,128)S(1)} %fusion.6), kind=kOutput, calls=%fused_computation.42 | convolution fusion | flops 402653184 | bytes 4198400 | tf_op jit(solution)/shard_map/dot_general | solution.py:56
  114.3 35.6 %psum.14 = f32[32,32]{0,1:T(8,128)S(1)} all-reduce(f32[32,32]{0,1:T(8,128)S(1)} %convolution_bitcast_fusion), channel_id=1, replica_groups=mesh['gx'=4,'gy'=8] {'gy'}, use_global_device_ids=true, to_apply=%region_0.1 | all-reduce | flops 1024 | bytes 8192 | tf_op jit(solution)/shard_map/psum | solution.py:59
  149.8 10.3 %psum.15 = f32[32,32]{0,1:T(8,128)S(1)} all-reduce(f32[32,32]{0,1:T(8,128)S(1)} %psum.14), channel_id=1, replica_groups=mesh['gx'=4,'gy'=8] {'gx'}, use_global_device_ids=true, to_apply=%region_1.2 | all-reduce | flops 1024 | bytes 8192 | tf_op jit(solution)/shard_map/psum | solution.py:59
  160.3 2.9 %cholesky.16 = f32[32,32]{1,0:T(8,128)S(1)} custom-call(f32[32,32]{1,0:T(8,128)S(1)} %fusion.27), custom_call_target="Cholesky" | custom-call | tf_op jit(solution)/shard_map/jit(cholesky)/cholesky | solution.py:60
  163.2 0.6 compare_reduce_fusion
  163.9 0.7 fusion.28
  164.5 0.7 copy.46
  165.2 2.4 %custom-call.7 = f32[1,32,32]{1,2,0:T(8,128)S(1)} custom-call(f32[1,32,32]{2,1,0:T(8,128)S(1)} %get-tuple-element.26), custom_call_target="InvertDiagBlocksLowerTriangular" | custom-call | tf_op jit(solution)/shard_map/jit(_solve_triangular)/triangular_solve | solution.py:61
  167.6 4.6 %copy.52 = f32[4,8,128,256]{3,2,1,0:T(8,128)S(1)} copy(f32[4,8,128,256]{3,1,0,2:T(8,128)} %bitcast.37) | data formatting | bytes 8388608
  172.3 5.9 %fusion.24 = f32[32,16,8,256]{3,0,2,1:T(8,128)S(1)} fusion(f32[16,8,256,32]{2,1,0,3:T(8,128)S(1)} %bitcast.38, f32[1,32,32]{1,2,0:T(8,128)S(1)} %custom-call.7), kind=kOutput, calls=%fused_computation.40 | convolution fusion | flops 402653184 | bytes 8392704 | tf_op jit(solution)/shard_map/jit(_solve_triangular)/triangular_solve | solution.py:61
  178.2 4.4 %copy.45 = f32[32,16,8,256]{3,2,1,0:T(8,128)} copy(f32[32,16,8,256]{3,0,2,1:T(8,128)S(1)} %fusion.24) | data formatting | bytes 8388608
  (22 shorter events, 0.4 us)
Async XLA Ops:
  0.6 8.5 %copy-start.2 = (f32[32,16,8,256]{3,2,1,0:T(8,128)S(1)}, f32[32,16,8,256]{3,2,1,0:T(8,128)}, u32[]{:S(2)}) copy-start(f32[32,16,8,256]{3,2,1,0:T(8,128)} %param.3) | copy-start | bytes 12582916
  5.5 3.7 %collective-permute-start.1 = (f32[32,1,8,256]{3,0,2,1:T(8,128)S(1)}, f32[32,1,8,256]{3,0,2,1:T(8,128)S(1)}, u32[]{:S(2)}, u32[]{:S(2)}) collective-permute-start(f32[32,1,8,256]{3,0,2,1:T(8,128)S(1)} %get-tuple-element.17), channel_id=1, source_target_pairs={{0,8},{8,16},{16,24},{1,9},{9,17},{17,25},{2,10},{10,18},{18,26},{... | collective-permute-start | bytes 786440 | tf_op jit(solution)/shard_map/ppermute | solution.py:17
  7.8 5.5 %collective-permute-start = (f32[32,1,8,256]{3,0,2,1:T(8,128)S(1)}, f32[32,1,8,256]{3,0,2,1:T(8,128)S(1)}, u32[]{:S(2)}, u32[]{:S(2)}) collective-permute-start(f32[32,1,8,256]{3,0,2,1:T(8,128)S(1)} %get-tuple-element.16), channel_id=1, source_target_pairs={{8,0},{16,8},{24,16},{9,1},{17,9},{25,17},{10,2},{18,10},{26,18},{... | collective-permute-start | bytes 786440 | tf_op jit(solution)/shard_map/ppermute | solution.py:19
  9.2 10.2 %copy-start.4 = (f32[3,16,8,256]{3,2,1,0:T(8,128)S(1)}, f32[3,16,8,256]{3,2,1,0:T(8,128)}, u32[]{:S(2)}) copy-start(f32[3,16,8,256]{3,2,1,0:T(8,128)} %param.5) | copy-start | bytes 1179652
  9.2 10.2 %copy-start.5 = (f32[16,8,256]{2,1,0:T(8,128)S(1)}, f32[16,8,256]{2,1,0:T(8,128)}, u32[]{:S(2)}) copy-start(f32[16,8,256]{2,1,0:T(8,128)} %param.4) | copy-start | bytes 393220
  13.4 30.7 %copy-start.3 = (f32[32,18,8,256]{3,0,2,1:T(8,128)}, f32[32,18,8,256]{3,0,2,1:T(8,128)S(1)}, u32[]{:S(2)}) copy-start(f32[32,18,8,256]{3,0,2,1:T(8,128)S(1)} %constant_dynamic-update-slice_fusion) | copy-start | bytes 14155780
  13.5 14.2 %collective-permute-start.2 = (f32[32,18,1,256]{3,0,2,1:T(8,128)S(1)}, f32[32,18,1,256]{3,0,2,1:T(8,128)S(1)}, u32[]{:S(2)}, u32[]{:S(2)}) collective-permute-start(f32[32,18,1,256]{3,0,2,1:T(8,128)S(1)} %get-tuple-element.12), channel_id=1, source_target_pairs={{1,0},{2,1},{3,2},{4,3},{5,4},{6,5},{7,6},{9,8},{10,9},{11,10},{12... | collective-permute-start | bytes 1769480 | tf_op jit(solution)/shard_map/ppermute | solution.py:19
  14.8 29.3 %collective-permute-start.3 = (f32[32,18,1,256]{3,0,2,1:T(8,128)S(1)}, f32[32,18,1,256]{3,0,2,1:T(8,128)S(1)}, u32[]{:S(2)}, u32[]{:S(2)}) collective-permute-start(f32[32,18,1,256]{3,0,2,1:T(8,128)S(1)} %get-tuple-element.13), channel_id=1, source_target_pairs={{0,1},{1,2},{2,3},{3,4},{4,5},{5,6},{6,7},{8,9},{9,10},{10,11},{11... | collective-permute-start | bytes 1769480 | tf_op jit(solution)/shard_map/ppermute | solution.py:17
  53.5 20.9 %copy-start.1 = (f32[32,16,8,256]{3,0,2,1:T(8,128)}, f32[32,16,8,256]{3,0,2,1:T(8,128)S(1)}, u32[]{:S(2)}) copy-start(f32[32,16,8,256]{3,0,2,1:T(8,128)S(1)} %fusion.2) | copy-start | bytes 12582916
  53.6 3.5 %collective-permute-start.5 = (f32[32,1,8,256]{3,0,2,1:T(8,128)S(1)}, f32[32,1,8,256]{3,0,2,1:T(8,128)S(1)}, u32[]{:S(2)}, u32[]{:S(2)}) collective-permute-start(f32[32,1,8,256]{3,0,2,1:T(8,128)S(1)} %get-tuple-element.14), channel_id=1, source_target_pairs={{0,8},{8,16},{16,24},{1,9},{9,17},{17,25},{2,10},{10,18},{18,26},{... | collective-permute-start | bytes 786440 | tf_op jit(solution)/shard_map/ppermute | solution.py:17
  55.8 4.1 %collective-permute-start.4 = (f32[32,1,8,256]{3,0,2,1:T(8,128)S(1)}, f32[32,1,8,256]{3,0,2,1:T(8,128)S(1)}, u32[]{:S(2)}, u32[]{:S(2)}) collective-permute-start(f32[32,1,8,256]{3,0,2,1:T(8,128)S(1)} %get-tuple-element.15), channel_id=1, source_target_pairs={{8,0},{16,8},{24,16},{9,1},{17,9},{25,17},{10,2},{18,10},{26,18},{... | collective-permute-start | bytes 786440 | tf_op jit(solution)/shard_map/ppermute | solution.py:19
  60.0 14.4 %collective-permute-start.6 = (f32[32,18,1,256]{3,0,2,1:T(8,128)S(1)}, f32[32,18,1,256]{3,0,2,1:T(8,128)S(1)}, u32[]{:S(2)}, u32[]{:S(2)}) collective-permute-start(f32[32,18,1,256]{3,0,2,1:T(8,128)S(1)} %get-tuple-element.10), channel_id=1, source_target_pairs={{1,0},{2,1},{3,2},{4,3},{5,4},{6,5},{7,6},{9,8},{10,9},{11,10},{12... | collective-permute-start | bytes 1769480 | tf_op jit(solution)/shard_map/ppermute | solution.py:19
  61.3 30.2 %collective-permute-start.7 = (f32[32,18,1,256]{3,0,2,1:T(8,128)S(1)}, f32[32,18,1,256]{3,0,2,1:T(8,128)S(1)}, u32[]{:S(2)}, u32[]{:S(2)}) collective-permute-start(f32[32,18,1,256]{3,0,2,1:T(8,128)S(1)} %get-tuple-element.11), channel_id=1, source_target_pairs={{0,1},{1,2},{2,3},{3,4},{4,5},{5,6},{6,7},{8,9},{9,10},{10,11},{11... | collective-permute-start | bytes 1769480 | tf_op jit(solution)/shard_map/ppermute | solution.py:17
  108.9 2.0 %copy-start = (f32[32,16,8,256]{3,0,2,1:T(8,128)}, f32[32,16,8,256]{3,0,2,1:T(8,128)S(1)}, u32[]{:S(2)}) copy-start(f32[32,16,8,256]{3,0,2,1:T(8,128)S(1)} %fusion.6) | copy-start | bytes 12582916
